TPU v7x, 128 devices: a whole 4x4x4 slice. The times are simulated.
128 devices in a mesh: blk: 8 (over x, y_hi), pts: 16 (over y_lo, z, core).
Axes of the slice: x: 4, y: 4 (y_hi: 2, y_lo: 2; y = y_hi * 2 + y_lo), z: 4, core: 2. Of those that a mesh axis runs over, the one named last changes fastest.
Arguments:
- point_feats: bfloat16 [1024, 128, 768], P(('blk', 'pts')), may hold values from -6 to 6
- point_pos: bfloat16 [1024, 3, 128], P(('blk', 'pts')), may hold values from 0 to 1
- anchor_pos: float32 [3, 2048], P(None, ('blk', 'pts')), may hold values from 0 to 1
- send_tiles: int32 [128, 16, 2], P(('blk', 'pts')), may hold values from 0 to 7
- nbr_slots: int32 [2048, 8], P(('blk', 'pts')), may hold values from 0 to 31
- nbr_counts: int32 [2048], P(('blk', 'pts')), may hold values from 1 to 8
- in_weight: bfloat16 [768, 768], replicated, may hold values from -0.21875 to 0.21875
- q_weight: bfloat16 [768, 768], replicated, may hold values from -3 to 3
- k_weight: bfloat16 [768, 768], replicated, may hold values from -3 to 3
- v_weight: bfloat16 [768, 768], replicated, may hold values from -0.21875 to 0.21875
- out_weight: bfloat16 [768, 768], replicated, may hold values from -0.21875 to 0.21875
- up_weight: bfloat16 [768, 3072], replicated, may hold values from -0.21875 to 0.21875
- down_weight: bfloat16 [3072, 768], replicated, may hold values from -0.109375 to 0.109375
Outputs:
- anchors_out: float32 [2048, 768], P(('blk', 'pts'))
- points_out: float32 [1024, 128, 768], P(('blk', 'pts'))
Inputs may be any that keep to these rules, and one draw needn't show every extreme that they name: `send_tiles`: local tile numbers within the sending group; a tile may be named for several owners or twice. `nbr_slots`: slot numbers q * 2 + k of the tiles that the anchor's group receives; entries at positions from nbr_counts on are padding.
All inputs are finite; a program needn't handle non-finite values.
Results may differ from a plain program's by a relative error of at most 0.017.
Values may be sent and summed in bfloat16 or wider, within the bound.
A program may use at most 128 MiB of HBM per device.

v0:
```python
import math

import jax
import jax.numpy as jnp
from jax import lax
from jax.sharding import PartitionSpec as P

HEADS = 12
HD = 64


RADIUS_SQUARED = 0.05
EPSILON = 1e-06


def rms_scaled(stream):
    return stream * lax.rsqrt(jnp.mean(stream * stream, axis=-1, keepdims=True) + EPSILON)


def pool_anchors(arrived, arrived_pos, centres, slot_lists, slot_counts):
    received = arrived.shape[0] * arrived.shape[1]
    tile_len = arrived.shape[2]
    arrived_rows = arrived.reshape(received * tile_len, arrived.shape[3])
    places = arrived_pos.astype(jnp.float32).reshape(received, 3, tile_len)
    offsets = places[None, :, :, :] - jnp.transpose(centres)[:, None, :, None]
    distance = jnp.sum(offsets * offsets, axis=2)
    kernel = 1.0 / (1.0 + distance / RADIUS_SQUARED)
    positions = jnp.arange(slot_lists.shape[1], dtype=jnp.int32)
    in_list = positions[None, :] < slot_counts[:, None]
    matches = (
        slot_lists[:, :, None] == jnp.arange(received, dtype=jnp.int32)[None, None, :]
    ) & in_list[:, :, None]
    picked = jnp.sum(matches.astype(jnp.float32), axis=1)
    pool_weights = (
        (picked[:, :, None] * kernel)
        .reshape(centres.shape[1], received * tile_len)
        .astype(jnp.bfloat16)
    )
    summed = jnp.dot(pool_weights, arrived_rows, preferred_element_type=jnp.float32)
    return summed / slot_counts.astype(jnp.float32)[:, None]


def finish_stream(stream, attended, out_weight, up_weight, down_weight):
    residual = stream + jnp.dot(attended, out_weight, preferred_element_type=jnp.float32)
    normed = rms_scaled(residual).astype(jnp.bfloat16)
    hidden = jax.nn.gelu(jnp.dot(normed, up_weight, preferred_element_type=jnp.float32)).astype(
        jnp.bfloat16
    )
    return residual + jnp.dot(hidden, down_weight, preferred_element_type=jnp.float32)


def attend_block(state_now, queries, key_rows, value_rows):
    running_max, totals, accumulated = state_now
    score_scale = 1.0 / math.sqrt(HD)
    scores = (
        jnp.einsum("qhd,khd->hqk", queries, key_rows, preferred_element_type=jnp.float32)
        * score_scale
    )
    fresh_max = jnp.maximum(running_max, jnp.max(scores, axis=-1))
    factor = jnp.exp(running_max - fresh_max)
    weights = jnp.exp(scores - fresh_max[:, :, None])
    totals = totals * factor + jnp.sum(weights, axis=-1)
    update = jnp.einsum(
        "hqk,khd->qhd", weights.astype(jnp.bfloat16), value_rows, preferred_element_type=jnp.float32
    )
    accumulated = accumulated * jnp.transpose(factor)[:, :, None] + update
    return (fresh_max, totals, accumulated)


def make_folder(queries):

    def fold_keys(state_now, shard_rows, first_row):
        key_rows = shard_rows[0]
        value_rows = shard_rows[1]
        row_count = key_rows.shape[0]
        block_rows = math.gcd(row_count, 256)
        blocks = row_count // block_rows
        key_blocks = key_rows.reshape(blocks, block_rows, HEADS, HD)
        value_blocks = value_rows.reshape(blocks, block_rows, HEADS, HD)

        def advance(state_inner, block_pair):
            return (attend_block(state_inner, queries, block_pair[0], block_pair[1]), None)

        state_now, _ignored = lax.scan(advance, state_now, (key_blocks, value_blocks))
        return state_now

    return fold_keys


def body(
    point_feats,
    point_pos,
    anchor_pos,
    send_tiles,
    nbr_slots,
    nbr_counts,
    in_weight,
    q_weight,
    k_weight,
    v_weight,
    out_weight,
    up_weight,
    down_weight,
):
    tiles_here, tile_len, feature_width = point_feats.shape
    point_count = tiles_here * tile_len
    anchor_count = anchor_pos.shape[1]
    embedded = jnp.dot(
        point_feats.reshape(point_count, feature_width),
        in_weight,
        preferred_element_type=jnp.float32,
    ).astype(jnp.bfloat16)
    chosen = send_tiles[0]
    outgoing = jnp.take(embedded.reshape(tiles_here, tile_len, feature_width), chosen, axis=0)
    outgoing_pos = jnp.take(point_pos, chosen, axis=0)
    arrived, arrived_pos = (
        lax.all_to_all(outgoing, "pts", split_axis=0, concat_axis=0, tiled=True),
        lax.all_to_all(outgoing_pos, "pts", split_axis=0, concat_axis=0, tiled=True),
    )
    pooled = pool_anchors(arrived, arrived_pos, anchor_pos, nbr_slots, nbr_counts)
    point_stream = embedded.astype(jnp.float32)
    point_normed = rms_scaled(point_stream).astype(jnp.bfloat16)
    point_queries = jnp.dot(point_normed, q_weight, preferred_element_type=jnp.float32).astype(
        jnp.bfloat16
    )
    anchor_normed = rms_scaled(pooled).astype(jnp.bfloat16)
    anchor_queries = jnp.dot(anchor_normed, q_weight, preferred_element_type=jnp.float32).astype(
        jnp.bfloat16
    )
    stream = jnp.concatenate([pooled, point_stream], axis=0)
    total_rows = anchor_count + point_count
    queries = jnp.concatenate([anchor_queries, point_queries], axis=0).reshape(
        total_rows, HEADS, HD
    )
    key_rows = jnp.dot(anchor_normed, k_weight, preferred_element_type=jnp.float32).astype(
        jnp.bfloat16
    )
    value_rows = jnp.dot(anchor_normed, v_weight, preferred_element_type=jnp.float32).astype(
        jnp.bfloat16
    )
    moving = jnp.stack([key_rows, value_rows])
    fold_keys = make_folder(queries)
    initial = (
        jnp.full((HEADS, total_rows), -jnp.inf, jnp.float32),
        jnp.zeros((HEADS, total_rows), jnp.float32),
        jnp.zeros((total_rows, HEADS, HD), jnp.float32),
    )
    running_max, totals, accumulated = fold_keys(
        initial, lax.all_gather(moving, ("blk", "pts"), axis=1, tiled=True), jnp.int32(0)
    )
    attended = (
        (accumulated / jnp.transpose(totals)[:, :, None])
        .reshape(total_rows, feature_width)
        .astype(jnp.bfloat16)
    )
    finished = finish_stream(stream, attended, out_weight, up_weight, down_weight)
    return (
        finished[:anchor_count],
        finished[anchor_count:].reshape(tiles_here, tile_len, feature_width),
    )


def solution(mesh):
    return jax.shard_map(
        body,
        mesh=mesh,
        in_specs=(
            P(("blk", "pts"), None, None),
            P(("blk", "pts"), None, None),
            P(None, ("blk", "pts")),
            P(("blk", "pts"), None, None),
            P(("blk", "pts"), None),
            P(("blk", "pts")),
            P(),
            P(),
            P(),
            P(),
            P(),
            P(),
            P(),
        ),
        out_specs=(P(("blk", "pts"), None), P(("blk", "pts"), None, None)),
        check_vma=False,
    )
```

profile of v0, /device:TPU:1, one launch (start us, length us, event | category | flops | bytes accessed | tf_op | source)
XLA Modules:
  0.0 448.1 jit_solution(3079787109022942670)
XLA Ops:
  11.0 7.8 %all-to-all-start = ((bf16[16,2,3,128]{3,1,2,0:T(2,128)(2,1)}), bf16[16,2,3,128]{3,1,2,0:T(2,128)(2,1)S(1)}, u32[]{:S(2)}, u32[]{:S(2)}) async-start(bf16[16,2,3,128]{3,1,2,0:T(2,128)(2,1)} %broadcast_select_fusion.1), calls=%async_computation | async-start | bytes 49152 | tf_op jit(solution)/shard_map/all_to_all | solution.py:118
  25.2 6.1 %broadcast_select_fusion = bf16[16,2,128,768]{3,2,1,0:T(8,128)(2,1)} fusion(bf16[16,2,128,768]{3,2,1,0:T(8,128)(2,1)} %bitcast.106, pred[16,2]{1,0:T(8,128)(4,1)S(1)} %copy.72), kind=kLoop, calls=%fused_computation.35 | loop fusion | flops 3145728 | bytes 12582944 | tf_op jit(solution)/shard_map/jit(_take)/select_n | solution.py:114
  31.3 5.9 %all-to-all-start.1 = ((bf16[16,2,128,768]{3,2,1,0:T(8,128)(2,1)}), bf16[16,2,128,768]{3,2,1,0:T(8,128)(2,1)}, u32[]{:S(2)}, u32[]{:S(2)}) async-start(bf16[16,2,128,768]{3,2,1,0:T(8,128)(2,1)} %broadcast_select_fusion), calls=%async_computation.1 | async-start | bytes 12582912 | tf_op jit(solution)/shard_map/all_to_all | solution.py:117
  37.9 87.8 %all-to-all-done.1 = bf16[16,2,128,768]{3,2,1,0:T(8,128)(2,1)} async-done(((bf16[16,2,128,768]{3,2,1,0:T(8,128)(2,1)}), bf16[16,2,128,768]{3,2,1,0:T(8,128)(2,1)}, u32[]{:S(2)}, u32[]{:S(2)}) %all-to-all-start.1) | async-done | bytes 6291488 | tf_op jit(solution)/shard_map/all_to_all | solution.py:117
  138.7 68.0 %all-gather.2.cloned.1.call-done = bf16[2,2048,768]{2,1,0:T(8,128)(2,1)} async-done(((bf16[2,16,768]{2,1,0:T(8,128)(2,1)}), bf16[2,2048,768]{2,1,0:T(8,128)(2,1)}) %all-gather.2.cloned.1.call-update) | async-done | bytes 6291472 | tf_op jit(solution)/shard_map/all_gather | solution.py:149
  206.7 6.0 %fusion.39 = (bf16[1,2048,768]{2,1,0:T(8,128)(2,1)}, bf16[1,2048,768]{2,1,0:T(8,128)(2,1)}) fusion(bf16[2,2048,768]{2,1,0:T(8,128)(2,1)} %all-gather.2.cloned.1.call-done), kind=kLoop, calls=%fused_computation.75 | loop fusion | bytes 12582912 | tf_op jit(solution)/shard_map/slice | solution.py:74
  232.8 178.8 %while.15 = (s32[]{:T(128)}, f32[12,1040]{1,0:T(8,128)S(1)}, f32[12,1040]{1,0:T(8,128)S(1)}, f32[1040,12,64]{0,2,1:T(8,128)}, bf16[8,256,12,64]{1,3,2,0:T(8,128)...) while((s32[]{:T(128)}, f32[12,1040]{1,0:T(8,128)S(1)}, ...), condition=%wide.region_7.8_spmd.clone, body=%wide.region_4.7_spmd.clone.sunk | while | flops 845919360 | bytes 99374208 | solution.py:84
  232.8 7.6 %bitcast_reduce_fusion.2 = (f32[12,1040]{1,0:T(8,128)S(1)}, f32[12,256,1040]{1,2,0:T(8,128)}) fusion(bf16[1040,12,64]{0,2,1:T(8,128)(2,1)S(1)} %get-tuple-element.208, bf16[8,256,12,64]{1,3,2,0:T(8,128)(2,1)} %get-tuple-element.207, s32[]{:T(128)} %get-tuple-element.194), kind=kOutput, calls=%fused_computation.3.clone.1 | convolution fusion | flops 415321920 | bytes 14820608 | tf_op jit(solution)/shard_map/while/body/eval_jaxpr/qhd,khd->hqk/dot_general | solution.py:56
  240.4 8.4 %fusion.73 = f32[1040,12,64]{0,2,1:T(8,128)} fusion(f32[12,256,1040]{1,2,0:T(8,128)} %get-tuple-element.183, f32[12,1040]{1,0:T(8,128)S(1)} %get-tuple-element.204, f32[1040,12,64]{0,2,1:T(8,128)} %get-tuple-element.197, f32[1040,12]{0,1:T(8,128)S(1)} %get-tuple-element.184, pred[]{:T(512)S(6)} %compare.3, ...), kind=kOutput, calls=%fused_computation.11.clone.1 | convolution fusion | flops 420925440 | bytes 20006912 | tf_op jit(solution)/shard_map/while/body/eval_jaxpr/hqk,khd->qhd/dot_general | solution.py:63
  254.3 7.6 %bitcast_reduce_fusion.2 = (f32[12,1040]{1,0:T(8,128)S(1)}, f32[12,256,1040]{1,2,0:T(8,128)}) fusion(bf16[1040,12,64]{0,2,1:T(8,128)(2,1)S(1)} %get-tuple-element.208, bf16[8,256,12,64]{1,3,2,0:T(8,128)(2,1)} %get-tuple-element.207, s32[]{:T(128)} %get-tuple-element.194), kind=kOutput, calls=%fused_computation.3.clone.1 | convolution fusion | flops 415321920 | bytes 14820608 | tf_op jit(solution)/shard_map/while/body/eval_jaxpr/qhd,khd->hqk/dot_general | solution.py:56
  261.9 8.6 %fusion.73 = f32[1040,12,64]{0,2,1:T(8,128)} fusion(f32[12,256,1040]{1,2,0:T(8,128)} %get-tuple-element.183, f32[12,1040]{1,0:T(8,128)S(1)} %get-tuple-element.204, f32[1040,12,64]{0,2,1:T(8,128)} %get-tuple-element.197, f32[1040,12]{0,1:T(8,128)S(1)} %get-tuple-element.184, pred[]{:T(512)S(6)} %compare.3, ...), kind=kOutput, calls=%fused_computation.11.clone.1 | convolution fusion | flops 420925440 | bytes 20006912 | tf_op jit(solution)/shard_map/while/body/eval_jaxpr/hqk,khd->qhd/dot_general | solution.py:63
  276.7 7.6 %bitcast_reduce_fusion.2 = (f32[12,1040]{1,0:T(8,128)S(1)}, f32[12,256,1040]{1,2,0:T(8,128)}) fusion(bf16[1040,12,64]{0,2,1:T(8,128)(2,1)S(1)} %get-tuple-element.208, bf16[8,256,12,64]{1,3,2,0:T(8,128)(2,1)} %get-tuple-element.207, s32[]{:T(128)} %get-tuple-element.194), kind=kOutput, calls=%fused_computation.3.clone.1 | convolution fusion | flops 415321920 | bytes 14820608 | tf_op jit(solution)/shard_map/while/body/eval_jaxpr/qhd,khd->hqk/dot_general | solution.py:56
  284.3 8.6 %fusion.73 = f32[1040,12,64]{0,2,1:T(8,128)} fusion(f32[12,256,1040]{1,2,0:T(8,128)} %get-tuple-element.183, f32[12,1040]{1,0:T(8,128)S(1)} %get-tuple-element.204, f32[1040,12,64]{0,2,1:T(8,128)} %get-tuple-element.197, f32[1040,12]{0,1:T(8,128)S(1)} %get-tuple-element.184, pred[]{:T(512)S(6)} %compare.3, ...), kind=kOutput, calls=%fused_computation.11.clone.1 | convolution fusion | flops 420925440 | bytes 20006912 | tf_op jit(solution)/shard_map/while/body/eval_jaxpr/hqk,khd->qhd/dot_general | solution.py:63
  299.2 7.6 %bitcast_reduce_fusion.2 = (f32[12,1040]{1,0:T(8,128)S(1)}, f32[12,256,1040]{1,2,0:T(8,128)}) fusion(bf16[1040,12,64]{0,2,1:T(8,128)(2,1)S(1)} %get-tuple-element.208, bf16[8,256,12,64]{1,3,2,0:T(8,128)(2,1)} %get-tuple-element.207, s32[]{:T(128)} %get-tuple-element.194), kind=kOutput, calls=%fused_computation.3.clone.1 | convolution fusion | flops 415321920 | bytes 14820608 | tf_op jit(solution)/shard_map/while/body/eval_jaxpr/qhd,khd->hqk/dot_general | solution.py:56
  306.8 8.6 %fusion.73 = f32[1040,12,64]{0,2,1:T(8,128)} fusion(f32[12,256,1040]{1,2,0:T(8,128)} %get-tuple-element.183, f32[12,1040]{1,0:T(8,128)S(1)} %get-tuple-element.204, f32[1040,12,64]{0,2,1:T(8,128)} %get-tuple-element.197, f32[1040,12]{0,1:T(8,128)S(1)} %get-tuple-element.184, pred[]{:T(512)S(6)} %compare.3, ...), kind=kOutput, calls=%fused_computation.11.clone.1 | convolution fusion | flops 420925440 | bytes 20006912 | tf_op jit(solution)/shard_map/while/body/eval_jaxpr/hqk,khd->qhd/dot_general | solution.py:63
  321.6 7.6 %bitcast_reduce_fusion.2 = (f32[12,1040]{1,0:T(8,128)S(1)}, f32[12,256,1040]{1,2,0:T(8,128)}) fusion(bf16[1040,12,64]{0,2,1:T(8,128)(2,1)S(1)} %get-tuple-element.208, bf16[8,256,12,64]{1,3,2,0:T(8,128)(2,1)} %get-tuple-element.207, s32[]{:T(128)} %get-tuple-element.194), kind=kOutput, calls=%fused_computation.3.clone.1 | convolution fusion | flops 415321920 | bytes 14820608 | tf_op jit(solution)/shard_map/while/body/eval_jaxpr/qhd,khd->hqk/dot_general | solution.py:56
  329.2 8.6 %fusion.73 = f32[1040,12,64]{0,2,1:T(8,128)} fusion(f32[12,256,1040]{1,2,0:T(8,128)} %get-tuple-element.183, f32[12,1040]{1,0:T(8,128)S(1)} %get-tuple-element.204, f32[1040,12,64]{0,2,1:T(8,128)} %get-tuple-element.197, f32[1040,12]{0,1:T(8,128)S(1)} %get-tuple-element.184, pred[]{:T(512)S(6)} %compare.3, ...), kind=kOutput, calls=%fused_computation.11.clone.1 | convolution fusion | flops 420925440 | bytes 20006912 | tf_op jit(solution)/shard_map/while/body/eval_jaxpr/hqk,khd->qhd/dot_general | solution.py:63
  344.1 7.6 %bitcast_reduce_fusion.2 = (f32[12,1040]{1,0:T(8,128)S(1)}, f32[12,256,1040]{1,2,0:T(8,128)}) fusion(bf16[1040,12,64]{0,2,1:T(8,128)(2,1)S(1)} %get-tuple-element.208, bf16[8,256,12,64]{1,3,2,0:T(8,128)(2,1)} %get-tuple-element.207, s32[]{:T(128)} %get-tuple-element.194), kind=kOutput, calls=%fused_computation.3.clone.1 | convolution fusion | flops 415321920 | bytes 14820608 | tf_op jit(solution)/shard_map/while/body/eval_jaxpr/qhd,khd->hqk/dot_general | solution.py:56
  351.7 8.6 %fusion.73 = f32[1040,12,64]{0,2,1:T(8,128)} fusion(f32[12,256,1040]{1,2,0:T(8,128)} %get-tuple-element.183, f32[12,1040]{1,0:T(8,128)S(1)} %get-tuple-element.204, f32[1040,12,64]{0,2,1:T(8,128)} %get-tuple-element.197, f32[1040,12]{0,1:T(8,128)S(1)} %get-tuple-element.184, pred[]{:T(512)S(6)} %compare.3, ...), kind=kOutput, calls=%fused_computation.11.clone.1 | convolution fusion | flops 420925440 | bytes 20006912 | tf_op jit(solution)/shard_map/while/body/eval_jaxpr/hqk,khd->qhd/dot_general | solution.py:63
  366.5 7.6 %bitcast_reduce_fusion.2 = (f32[12,1040]{1,0:T(8,128)S(1)}, f32[12,256,1040]{1,2,0:T(8,128)}) fusion(bf16[1040,12,64]{0,2,1:T(8,128)(2,1)S(1)} %get-tuple-element.208, bf16[8,256,12,64]{1,3,2,0:T(8,128)(2,1)} %get-tuple-element.207, s32[]{:T(128)} %get-tuple-element.194), kind=kOutput, calls=%fused_computation.3.clone.1 | convolution fusion | flops 415321920 | bytes 14820608 | tf_op jit(solution)/shard_map/while/body/eval_jaxpr/qhd,khd->hqk/dot_general | solution.py:56
  374.1 8.6 %fusion.73 = f32[1040,12,64]{0,2,1:T(8,128)} fusion(f32[12,256,1040]{1,2,0:T(8,128)} %get-tuple-element.183, f32[12,1040]{1,0:T(8,128)S(1)} %get-tuple-element.204, f32[1040,12,64]{0,2,1:T(8,128)} %get-tuple-element.197, f32[1040,12]{0,1:T(8,128)S(1)} %get-tuple-element.184, pred[]{:T(512)S(6)} %compare.3, ...), kind=kOutput, calls=%fused_computation.11.clone.1 | convolution fusion | flops 420925440 | bytes 20006912 | tf_op jit(solution)/shard_map/while/body/eval_jaxpr/hqk,khd->qhd/dot_general | solution.py:63
  389.0 7.6 %bitcast_reduce_fusion.2 = (f32[12,1040]{1,0:T(8,128)S(1)}, f32[12,256,1040]{1,2,0:T(8,128)}) fusion(bf16[1040,12,64]{0,2,1:T(8,128)(2,1)S(1)} %get-tuple-element.208, bf16[8,256,12,64]{1,3,2,0:T(8,128)(2,1)} %get-tuple-element.207, s32[]{:T(128)} %get-tuple-element.194), kind=kOutput, calls=%fused_computation.3.clone.1 | convolution fusion | flops 415321920 | bytes 14820608 | tf_op jit(solution)/shard_map/while/body/eval_jaxpr/qhd,khd->hqk/dot_general | solution.py:56
  396.6 8.6 %fusion.73 = f32[1040,12,64]{0,2,1:T(8,128)} fusion(f32[12,256,1040]{1,2,0:T(8,128)} %get-tuple-element.183, f32[12,1040]{1,0:T(8,128)S(1)} %get-tuple-element.204, f32[1040,12,64]{0,2,1:T(8,128)} %get-tuple-element.197, f32[1040,12]{0,1:T(8,128)S(1)} %get-tuple-element.184, pred[]{:T(512)S(6)} %compare.3, ...), kind=kOutput, calls=%fused_computation.11.clone.1 | convolution fusion | flops 420925440 | bytes 20006912 | tf_op jit(solution)/shard_map/while/body/eval_jaxpr/hqk,khd->qhd/dot_general | solution.py:63
  418.2 17.9 %convolution_add_fusion.1 = f32[1040,768]{1,0:T(8,128)} fusion(f32[1040,768]{1,0:T(8,128)} %get-tuple-element.133, bf16[3072,768]{1,0:T(8,128)(2,1)} %param.27, bf16[768,3072]{1,0:T(8,128)(2,1)} %param.26, f32[1040]{0:T(1024)S(1)} %add_rsqrt_fusion), kind=kOutput, calls=%fused_computation.37 | convolution fusion | flops 9845821440 | bytes 15831104 | tf_op jit(solution)/shard_map/dot_general | solution.py:49
  (116 shorter events, 104.9 us)
Async XLA Ops:
  7.2 11.7 %copy-start = (bf16[8,128,768]{2,1,0:T(8,128)(2,1)S(1)}, bf16[8,128,768]{2,1,0:T(8,128)(2,1)}, u32[]{:S(2)}) copy-start(bf16[8,128,768]{2,1,0:T(8,128)(2,1)} %param.15) | copy-start | bytes 4718596
  11.0 20.3 %all-to-all-start = ((bf16[16,2,3,128]{3,1,2,0:T(2,128)(2,1)}), bf16[16,2,3,128]{3,1,2,0:T(2,128)(2,1)S(1)}, u32[]{:S(2)}, u32[]{:S(2)}) async-start(bf16[16,2,3,128]{3,1,2,0:T(2,128)(2,1)} %broadcast_select_fusion.1), calls=%async_computation | async-start | bytes 49152 | tf_op jit(solution)/shard_map/all_to_all | solution.py:118
  31.3 5.9 %copy-start.8 = (f32[3,16]{1,0:T(4,128)S(1)}, f32[3,16]{1,0:T(4,128)}, u32[]{:S(2)}) copy-start(f32[3,16]{1,0:T(4,128)} %param.17) | copy-start | bytes 580
  31.3 6.0 %copy-start.7 = (s32[16,8]{0,1:T(8,128)S(1)}, s32[16,8]{0,1:T(8,128)}, u32[]{:S(2)}) copy-start(s32[16,8]{0,1:T(8,128)} %param.19) | copy-start | bytes 1540
  31.3 6.1 %copy-start.9 = (s32[16]{0:T(128)S(1)}, s32[16]{0:T(128)}, u32[]{:S(2)}) copy-start(s32[16]{0:T(128)} %param.20) | copy-start | bytes 196
  31.3 94.4 %all-to-all-start.1 = ((bf16[16,2,128,768]{3,2,1,0:T(8,128)(2,1)}), bf16[16,2,128,768]{3,2,1,0:T(8,128)(2,1)}, u32[]{:S(2)}, u32[]{:S(2)}) async-start(bf16[16,2,128,768]{3,2,1,0:T(8,128)(2,1)} %broadcast_select_fusion), calls=%async_computation.1 | async-start | bytes 12582912 | tf_op jit(solution)/shard_map/all_to_all | solution.py:117
  37.2 169.5 %all-gather.2.cloned.1.call-start = ((), (), s32[]{:S(2)}) async-start(), calls=%async_computation.2 | async-start | bytes 6340608 | tf_op jit(solution)/shard_map/all_gather | solution.py:149
  125.7 4.1 copy-start.4
  125.7 4.3 copy-start.5
  130.1 2.9 copy-start.6
  240.4 9.7 %copy-start.2 = (f32[12,256,1040]{1,2,0:T(8,128)S(1)}, f32[12,256,1040]{1,2,0:T(8,128)}, u32[]{:S(2)}) copy-start(f32[12,256,1040]{1,2,0:T(8,128)} %get-tuple-element.183) | copy-start | bytes 38338564 | tf_op jit(solution)/shard_map/while
  261.9 10.7 %copy-start.2 = (f32[12,256,1040]{1,2,0:T(8,128)S(1)}, f32[12,256,1040]{1,2,0:T(8,128)}, u32[]{:S(2)}) copy-start(f32[12,256,1040]{1,2,0:T(8,128)} %get-tuple-element.183) | copy-start | bytes 38338564 | tf_op jit(solution)/shard_map/while
  284.3 10.7 %copy-start.2 = (f32[12,256,1040]{1,2,0:T(8,128)S(1)}, f32[12,256,1040]{1,2,0:T(8,128)}, u32[]{:S(2)}) copy-start(f32[12,256,1040]{1,2,0:T(8,128)} %get-tuple-element.183) | copy-start | bytes 38338564 | tf_op jit(solution)/shard_map/while
  306.8 10.7 %copy-start.2 = (f32[12,256,1040]{1,2,0:T(8,128)S(1)}, f32[12,256,1040]{1,2,0:T(8,128)}, u32[]{:S(2)}) copy-start(f32[12,256,1040]{1,2,0:T(8,128)} %get-tuple-element.183) | copy-start | bytes 38338564 | tf_op jit(solution)/shard_map/while
  329.2 10.7 %copy-start.2 = (f32[12,256,1040]{1,2,0:T(8,128)S(1)}, f32[12,256,1040]{1,2,0:T(8,128)}, u32[]{:S(2)}) copy-start(f32[12,256,1040]{1,2,0:T(8,128)} %get-tuple-element.183) | copy-start | bytes 38338564 | tf_op jit(solution)/shard_map/while
  351.7 10.7 %copy-start.2 = (f32[12,256,1040]{1,2,0:T(8,128)S(1)}, f32[12,256,1040]{1,2,0:T(8,128)}, u32[]{:S(2)}) copy-start(f32[12,256,1040]{1,2,0:T(8,128)} %get-tuple-element.183) | copy-start | bytes 38338564 | tf_op jit(solution)/shard_map/while
  374.1 10.7 %copy-start.2 = (f32[12,256,1040]{1,2,0:T(8,128)S(1)}, f32[12,256,1040]{1,2,0:T(8,128)}, u32[]{:S(2)}) copy-start(f32[12,256,1040]{1,2,0:T(8,128)} %get-tuple-element.183) | copy-start | bytes 38338564 | tf_op jit(solution)/shard_map/while
  396.6 10.7 %copy-start.2 = (f32[12,256,1040]{1,2,0:T(8,128)S(1)}, f32[12,256,1040]{1,2,0:T(8,128)}, u32[]{:S(2)}) copy-start(f32[12,256,1040]{1,2,0:T(8,128)} %get-tuple-element.183) | copy-start | bytes 38338564 | tf_op jit(solution)/shard_map/while
  411.7 3.0 copy-start.3
  411.7 3.3 copy-start.10
  418.2 23.1 %copy-start.1 = (bf16[8,128,768]{2,1,0:T(8,128)(2,1)S(1)}, bf16[8,128,768]{2,1,0:T(8,128)(2,1)}, u32[]{:S(2)}) copy-start(bf16[8,128,768]{2,1,0:T(8,128)(2,1)} %param.15) | copy-start | bytes 4718596
Sparse Core Ops, SparseCore 0:
  131.2 75.5 all-gather.1
where the time goes:
time: 449 us; the launch traced here: 448 us
  matrix products  159 us (35%)
  waiting for transfers between devices  156 us (35%)
  local copies, waits for them, and re-layouts  56.3 us (13%)
  other arithmetic  48.3 us (11%)
  between operations  14.2 us (3%)
  starting transfers between devices  13.7 us (3%)
    all_to_all x1, waiting for transfers between devices, body(): lax.all_to_all(outgoing, 'pts', split_axis=0, concat_axis=0, tiled=True)  87.8 us
    dot_general x8, matrix products, attend_block(): jnp.einsum('hqk,khd->qhd', weights.astype(jnp.bfloat16), value_rows, pref...  68.5 us
    all_gather x1, waiting for transfers between devices, body(): lax.all_gather(moving, ('blk', 'pts'), axis=1, tiled=True)  68 us
    dot_general x8, matrix products, attend_block(): jnp.einsum('qhd,khd->hqk', queries, key_rows, preferred_element_type=jnp....  60.5 us
    reduce_sum x8, other arithmetic, attend_block(): totals = totals * factor + jnp.sum(weights, axis=-1)  32.6 us
    dot_general x1, matrix products, finish_stream(): jnp.dot(hidden, down_weight, preferred_element_type=jnp.float32)  17.9 us
    while x24, local copies, waits for them, and re-layouts  16.1 us
    unnamed x25, local copies, waits for them, and re-layouts  11.6 us
  transfers between devices with their start and end apart: 3, of which 2 were waited for; matrix products, arithmetic and copies ran while one was open for 5% of the time, Pallas kernels for 0%

commit v1 on v0

v1 whole, which is shorter than its diff:
```python
import jax, jax.numpy as jnp
from jax import lax
from jax.experimental import pallas as pl
from jax.experimental.pallas import tpu as pltpu
from jax.sharding import PartitionSpec as P

HEADS=12; HD=64; D=768; FFH=3072; A=2048
ROWS=208; EPS=1e-6
LOG2E=1.4426950408889634

def rms(x):
    return x*lax.rsqrt(jnp.mean(x*x,axis=-1,keepdims=True)+EPS)

def dot(a,b):
    return jnp.dot(a,b,preferred_element_type=jnp.float32)

def kern(emb, pooled, nrm, wq_h, wk_h, wv_h, wo_h, wu_h, wd_h, anc_out, pts_out,
         wq, wk, wv, wo, wu, wd, kt, va, xs, osc, att, sems, osem):
    i=pl.program_id(0); n=pl.num_programs(0)
    pairs=((wk_h,wk),(wv_h,wv),(wq_h,wq),(wo_h,wo),(wu_h,wu),(wd_h,wd))
    def cp(j):
        return pltpu.make_async_copy(pairs[j][0],pairs[j][1],sems.at[j])
    def ocopy(j,slot):
        return pltpu.make_async_copy(osc.at[slot],pts_out.at[pl.ds(j*ROWS,ROWS)],osem.at[slot])
    @pl.when(i==0)
    def _():
        for j in range(6): cp(j).start()
        cp(0).wait()
        lane=lax.broadcasted_iota(jnp.int32,(256,128),1)
        lo=lane<HD
        wkT=wk[...].T
        for c in range(0,A,256):
            acc=None
            acv=None
            for part in range(3):
                blk=nrm[c:c+256,part*256:part*256+256]
                t=lax.dot_general(wkT[:,part*256:part*256+256],blk,(((1,),(1,)),((),())),preferred_element_type=jnp.float32)
                acc=t if acc is None else acc+t
            kt[:,c:c+256]=acc.astype(jnp.bfloat16)
        cp(1).wait()
        one=jnp.ones((256,128),jnp.bfloat16); zero=jnp.zeros((256,128),jnp.bfloat16)
        for c in range(0,A,256):
            acv=None
            for part in range(3):
                blk=nrm[c:c+256,part*256:part*256+256]
                t=dot(blk,wv[part*256:part*256+256,:])
                acv=t if acv is None else acv+t
            v=acv.astype(jnp.bfloat16)
            for p in range(HEADS//2):
                vp=v[:,128*p:128*p+128]
                va[2*p,c:c+256,0:128]=jnp.where(lo,vp,zero)
                va[2*p,c:c+256,128:256]=jnp.where(lo,one,zero)
                va[2*p+1,c:c+256,0:128]=jnp.where(lo,zero,vp)
                va[2*p+1,c:c+256,128:256]=jnp.where(lo,zero,one)
        cp(2).wait(); cp(3).wait()
    @pl.when(i<n-1)
    def _():
        xs[...]=emb[pl.ds(pl.multiple_of(i*ROWS,16),ROWS),:].astype(jnp.float32)
    @pl.when(i==n-1)
    def _():
        xs[0:ROWS-16,:]=emb[1024-(ROWS-16):1024,:].astype(jnp.float32)
        xs[ROWS-16:ROWS,:]=pooled[...]
    x=xs[...]
    nx=rms(x).astype(jnp.bfloat16)
    q=(dot(nx,wq[...])*(LOG2E/8.0)).astype(jnp.bfloat16)
    lane=lax.broadcasted_iota(jnp.int32,(ROWS,128),1)
    lo=lane<HD
    for p in range(HEADS//2):
        qp=q[:,128*p:128*p+128]
        zero=jnp.zeros_like(qp)
        o=jnp.zeros((ROWS,256),jnp.float32)
        for a in range(2):
            qa=jnp.where(lo,qp,zero) if a==0 else jnp.where(lo,zero,qp)
            s=dot(qa,kt[128*p:128*p+128,:])
            m=jnp.max(s,axis=1,keepdims=True)
            w=jnp.exp2(s-m).astype(jnp.bfloat16)
            o=o+dot(w,va[2*p+a,:,:])
        att[:,128*p:128*p+128]=(o[:,0:128]/o[:,128:256]).astype(jnp.bfloat16)
    res=x+dot(att[...],wo[...])
    @pl.when(i==0)
    def _():
        cp(4).wait(); cp(5).wait()
    n2=rms(res).astype(jnp.bfloat16)
    FC=768
    acc=res
    for c in range(0,FFH,FC):
        h=jax.nn.gelu(dot(n2,wu[:,c:c+FC])).astype(jnp.bfloat16)
        acc=acc+dot(h,wd[c:c+FC,:])
    slot=lax.rem(i,2)
    @pl.when(i>=2)
    def _():
        ocopy(i-2,slot).wait()
    osc[slot]=acc
    @pl.when(i<n-1)
    def _():
        ocopy(i,slot).start()
    @pl.when(i==n-1)
    def _():
        c1=pltpu.make_async_copy(osc.at[slot,pl.ds(0,ROWS-16)],pts_out.at[pl.ds(1024-(ROWS-16),ROWS-16)],osem.at[2])
        c2=pltpu.make_async_copy(osc.at[slot,pl.ds(ROWS-16,16)],anc_out,osem.at[3])
        c1.start(); c2.start()
        ocopy(i-1,1-slot).wait()
        c1.wait(); c2.wait()

def compute(emb,pooled,nrm,wq,wk,wv,wo,wu,wd):
    n=1040//ROWS
    full=pl.BlockSpec(memory_space=pltpu.VMEM)
    anys=pl.BlockSpec(memory_space=pl.ANY)
    bf=jnp.bfloat16
    return pl.pallas_call(kern,grid=(n,),
      in_specs=[full,full,full]+[anys]*6, out_specs=[anys,anys],
      out_shape=[jax.ShapeDtypeStruct((16,D),jnp.float32),jax.ShapeDtypeStruct((1024,D),jnp.float32)],
      scratch_shapes=[pltpu.VMEM((D,D),bf)]*4+[pltpu.VMEM((D,FFH),bf),pltpu.VMEM((FFH,D),bf),
        pltpu.VMEM((D,A),bf),pltpu.VMEM((HEADS,A,256),bf),pltpu.VMEM((ROWS,D),jnp.float32),pltpu.VMEM((2,ROWS,D),jnp.float32),
        pltpu.VMEM((ROWS,D),bf),pltpu.SemaphoreType.DMA((6,)),pltpu.SemaphoreType.DMA((4,))],
      compiler_params=pltpu.CompilerParams(vmem_limit_bytes=60*2**20,dimension_semantics=("arbitrary",)),
    )(emb,pooled,nrm,wq,wk,wv,wo,wu,wd)


def body(point_feats, point_pos, anchor_pos, send_tiles, nbr_slots, nbr_counts, in_weight, q_weight, k_weight, v_weight,
         out_weight, up_weight, down_weight):
    feats = point_feats.reshape(1024, D)
    me = lax.axis_index("pts")
    counts = nbr_counts.astype(jnp.float32)
    info = jnp.concatenate([anchor_pos.T, counts[:, None], nbr_slots.astype(jnp.float32)], axis=1)
    info = lax.all_gather(info, "pts", axis=0, tiled=True)
    emb = dot(feats, in_weight).astype(jnp.bfloat16)
    slots = info[:, 4:12]
    live = jnp.arange(8, dtype=jnp.float32)[None, :] < info[:, 3:4]
    base = (2 * me).astype(jnp.float32)
    sent = jnp.repeat(send_tiles[0], 16, axis=0)
    tiles = jnp.arange(8, dtype=jnp.int32)[None, :]
    counted = 0.0
    for k in range(2):
        times = jnp.sum(((slots == base + k) & live).astype(jnp.float32), axis=1, keepdims=True)
        counted = counted + jnp.where(sent[:, k:k + 1] == tiles, times, 0.0)
    places = point_pos.astype(jnp.float32)
    offsets = places[None] - info[:, None, 0:3, None]
    distance = jnp.sum(offsets * offsets, axis=2)
    weights = (counted[:, :, None] / (1.0 + distance / 0.05)).reshape(256, 1024).astype(jnp.bfloat16)
    partial = dot(weights, emb).astype(jnp.bfloat16)
    arrived = lax.all_to_all(partial.reshape(16, 16, D), "pts", split_axis=0, concat_axis=0, tiled=True)
    pooled = jnp.sum(arrived.astype(jnp.float32), axis=0) / counts[:, None]
    normed = rms(pooled).astype(jnp.bfloat16)
    gathered = lax.all_gather(normed, ("blk", "pts"), axis=0, tiled=True)
    anchors, points = compute(emb, pooled, gathered, q_weight, k_weight, v_weight, out_weight, up_weight, down_weight)
    return anchors, points.reshape(8, 128, D)


def solution(mesh):
    both = ("blk", "pts")
    return jax.shard_map(
        body,
        mesh=mesh,
        in_specs=(P(both, None, None), P(both, None, None), P(None, both), P(both, None, None), P(both, None), P(both))
        + (P(),) * 7,
        out_specs=(P(both, None), P(both, None, None)),
        check_vma=False,
    )
```

time: 449 us -> 183 us (0.41)
  matrix products: 159 us -> 1.98 us
  waiting for transfers between devices: 156 us -> 65.9 us
  Pallas kernels: 0 us -> 60.7 us
  local copies, waits for them, and re-layouts: 56.3 us -> 1.27 us
  other arithmetic: 48.3 us -> 5.41 us
  blocking collectives: 0 us -> 33.7 us
  starting transfers between devices: 13.7 us -> 0.04 us
    dot_general x24 -> x2, matrix products: 159 us -> 1.98 us  [dot(): return jnp.dot(a, b, preferred_element_type=jnp.float32)]
    all_to_all x2 -> x0, waiting for transfers between devices: 87.8 us -> none  [the longest x1 87.8 us: body(): lax.all_to_all(outgoing, 'pts', split_axis=0, concat_axis=0, tiled=True)]
    pallas_call x0 -> x1, Pallas kernels: none -> 60.7 us  [compute(): pl.pallas_call(kern, grid=(n,), in_specs=[full, full, full] + [anys] * 6,...]
    reduce_sum x10 -> x4, other arithmetic: 32.8 us -> 1.34 us  [the longest x1 1.06 us: body(): distance = jnp.sum(offsets * offsets, axis=2)]
    all_gather x0 -> x1, blocking collectives: none -> 22.6 us  [body(): info = lax.all_gather(info, 'pts', axis=0, tiled=True)]
    slice x5 -> x3, local copies, waits for them, and re-layouts: 20.5 us -> 0.28 us  [the longest x1 0.18 us: body(): live = jnp.arange(8, dtype=jnp.float32)[None, :] < info[:, 3:4]]
    while x24 -> x0, local copies, waits for them, and re-layouts: 16.1 us -> none
    all_to_all x2 -> x0, starting transfers between devices: 13.7 us -> none  [the longest x1 7.84 us: body(): lax.all_to_all(outgoing_pos, 'pts', split_axis=0, concat_axis=0, tiled=True)]
  transfers between devices with their start and end apart: 3 -> 1, of which waited for: 2 -> 1; matrix products, arithmetic and copies ran while one was open for 5% -> 0% of each run, Pallas kernels for 0% -> 0%
where the time goes in v1:
time: 183 us
  waiting for transfers between devices  65.9 us (36%)
  Pallas kernels  60.7 us (33%)
  blocking collectives  33.7 us (18%)
  between operations  14.2 us (8%)
  other arithmetic  5.41 us (3%)
  matrix products  1.98 us (1%)
    all_gather x1, waiting for transfers between devices, body(): gathered = lax.all_gather(normed, ('blk', 'pts'), axis=0, tiled=True)  65.9 us
    pallas_call x1, Pallas kernels, compute(): pl.pallas_call(kern, grid=(n,), in_specs=[full, full, full] + [anys] * 6,...  60.7 us
    all_gather x1, blocking collectives, body(): info = lax.all_gather(info, 'pts', axis=0, tiled=True)  22.6 us
    all_to_all x1, blocking collectives, body(): lax.all_to_all(partial.reshape(16, 16, D), 'pts', split_axis=0, concat_ax...  11.1 us
  transfers between devices with their start and end apart: 1, of which 1 were waited for; matrix products, arithmetic and copies ran while one was open for 0% of the time, Pallas kernels for 0%

profile of v1, /device:TPU:1, one launch (start us, length us, event | category | flops | bytes accessed | tf_op | source)
XLA Modules:
  0.0 183.2 jit_solution(6730113141646725443)
XLA Ops:
  7.2 0.0 all-gather.2.cloned.1.call-start
  7.2 0.8 fusion.5
  8.0 0.7 convert_element_type.38
  8.7 0.7 pad_maximum_fusion
  9.4 0.1 copy.31
  9.5 22.6 %all_gather.6 = f32[256,12]{1,0:T(8,128)S(1)} all-gather(f32[16,12]{1,0:T(8,128)S(1)} %copy.31), channel_id=1, replica_groups=mesh['blk'=8,'pts'=16] {'pts'}, dimensions={0}, use_global_device_ids=true | all-gather | bytes 13056 | tf_op jit(solution)/shard_map/all_gather | solution.py:126
  32.1 0.2 slice_reduce_fusion
  32.3 0.1 slice.27
  32.4 0.7 convert_element_type.42
  33.1 0.7 broadcast_in_dim.33
  33.8 0.1 reshape.114
  33.9 0.1 copy.33
  34.0 1.1 multiply_reduce_fusion
  35.1 0.2 select_add_fusion
  35.3 0.3 divide_convert_fusion
  35.7 1.4 convolution_convert_fusion.emb
  37.1 0.6 convolution_convert_fusion.1
  37.7 11.1 %all_to_all.5 = bf16[16,16,768]{2,1,0:T(8,128)(2,1)S(1)} all-to-all(bf16[16,16,768]{2,1,0:T(8,128)(2,1)S(1)} %bitcast.22), channel_id=1, replica_groups=mesh['blk'=8,'pts'=16] {'pts'}, dimensions={0} | all-to-all | bytes 786432 | tf_op jit(solution)/shard_map/all_to_all | solution.py:142
  48.7 0.1 convert_reduce_fusion
  48.8 0.2 multiply_reduce_fusion.1
  49.0 0.7 multiply_convert_fusion
  49.7 0.0 all-gather.2.cloned.1.call-update
  49.7 65.9 %all-gather.2.cloned.1.call-done.nrm = bf16[2048,768]{1,0:T(8,128)(2,1)} async-done(((bf16[16,768]{1,0:T(8,128)(2,1)}), bf16[2048,768]{1,0:T(8,128)(2,1)}) %all-gather.2.cloned.1.call-update) | async-done | bytes 3145744 | tf_op jit(solution)/shard_map/all_gather | solution.py:145
  115.6 60.7 %shard_map.140 = (f32[16,768]{1,0:T(8,128)}, f32[1024,768]{1,0:T(8,128)}) custom-call(bf16[1024,768]{1,0:T(8,128)(2,1)} %copy-done.1, f32[16,768]{1,0:T(8,128)} %copy-done.2, bf16[2048,768]{1,0:T(8,128)(2,1)} %all-gather.2.cloned.1.call-done.nrm, bf16[768,768]{1,0:T(8,128)(2,1)} %wq_h.1, bf16[768,768]{1,0:T(8,128)(2,1)} %wk_h.1, bf16[768,768]{1,0:T(8,128)(2,1)} %wv_h.1, ...), custom_call_target="tpu_custom_call" | custom-call | tf_op jit(solution)/shard_map/pallas_call | solution.py:110
  (11 shorter events, 0.1 us)
Async XLA Ops:
  7.2 28.5 %copy-start = (bf16[8,128,768]{2,1,0:T(8,128)(2,1)S(1)}, bf16[8,128,768]{2,1,0:T(8,128)(2,1)}, u32[]{:S(2)}) copy-start(bf16[8,128,768]{2,1,0:T(8,128)(2,1)} %param.13) | copy-start | bytes 4718596
  7.2 108.4 %all-gather.2.cloned.1.call-start = ((), (), s32[]{:S(2)}) async-start(), calls=%async_computation.1 | async-start | bytes 3170304 | tf_op jit(solution)/shard_map/all_gather | solution.py:145
  33.9 1.7 copy-start.3
  37.1 11.7 %copy-start.1 = (bf16[1024,768]{1,0:T(8,128)(2,1)}, bf16[1024,768]{1,0:T(8,128)(2,1)S(1)}, u32[]{:S(2)}) copy-start(bf16[1024,768]{1,0:T(8,128)(2,1)S(1)} %convolution_convert_fusion.emb) | copy-start | bytes 4718596
  49.0 66.6 %copy-start.2 = (f32[16,768]{1,0:T(8,128)}, f32[16,768]{1,0:T(8,128)S(1)}, u32[]{:S(2)}) copy-start(f32[16,768]{1,0:T(8,128)S(1)} %get-tuple-element.9.pooled) | copy-start | bytes 147460
Sparse Core Ops, SparseCore 0:
  49.8 65.7 all-gather.1

commit v2 on v1

--- a/solution.py
+++ b/solution.py
@@ -33,7 +33,7 @@
             acc=None
             acv=None
             for part in range(3):
-                blk=nrm[c:c+256,part*256:part*256+256]
+                blk=nrm[part,c:c+256,:]
                 t=lax.dot_general(wkT[:,part*256:part*256+256],blk,(((1,),(1,)),((),())),preferred_element_type=jnp.float32)
                 acc=t if acc is None else acc+t
             kt[:,c:c+256]=acc.astype(jnp.bfloat16)
@@ -42,7 +42,7 @@
         for c in range(0,A,256):
             acv=None
             for part in range(3):
-                blk=nrm[c:c+256,part*256:part*256+256]
+                blk=nrm[part,c:c+256,:]
                 t=dot(blk,wv[part*256:part*256+256,:])
                 acv=t if acv is None else acv+t
             v=acv.astype(jnp.bfloat16)
@@ -117,33 +117,206 @@
     )(emb,pooled,nrm,wq,wk,wv,wo,wu,wd)
 
 
+CORES = 2
+RING = 4
+GROUP = 16
+
+
+def gather_kernel(
+    feats_hbm, win_hbm, pos_ref, apos_ref, send_ref, slots_ref, counts_ref,
+    emb_ref, pooled_ref, box_ref,
+    feats, win, flip, info, pweights, outgoing, incoming,
+    local_sem, info_send, info_recv, part_send, part_recv, box_send, box_recv, twin_send, twin_recv,
+):
+    blk = lax.axis_index("blk")
+    pts = lax.axis_index("pts")
+    x, y_hi = blk // 2, lax.rem(blk, 2)
+    core = lax.rem(pts, 2)
+    chip = pts // 2
+    z, y_lo = lax.rem(chip, 4), chip // 4
+    y = y_hi * 2 + y_lo
+    place = (x, y, z)
+
+    def device(spot, c):
+        return (spot[0] * 2 + spot[1] // 2, (lax.rem(spot[1], 2) * 4 + spot[2]) * 2 + c)
+
+    def ring(axis, step):
+        spot = list(place)
+        spot[axis] = lax.rem(place[axis] + step, RING)
+        return tuple(spot)
+
+    def mate(step):
+        return lax.rem(pts + step, GROUP)
+
+    load_feats = pltpu.make_async_copy(feats_hbm, feats, local_sem.at[0])
+    load_win = pltpu.make_async_copy(win_hbm, win, local_sem.at[1])
+    load_win.start()
+    load_feats.start()
+
+    barrier = pltpu.get_barrier_semaphore()
+
+    def greet(device_id):
+        pl.semaphore_signal(barrier, inc=1, device_id=device_id, device_id_type=pl.DeviceIdType.MESH)
+
+    for step in range(1, GROUP):
+        greet((blk, mate(step)))
+    for step in range(1, RING):
+        greet(device(ring(0, step), core))
+    across = lax.rem(y_hi + 1, 2)
+    for low in range(2):
+        greet((x * 2 + across, (low * 4 + z) * 2 + core))
+
+    flip[...] = jnp.zeros_like(flip)
+    flip[0:3, 0:16] = apos_ref[...]
+    flip[3:4, 0:16] = counts_ref[...].astype(jnp.float32)
+    flip[8:16, 0:16] = slots_ref[...].astype(jnp.float32)
+    turned = flip[...].T
+    info[pl.ds(pts, 1)] = turned[0:16, :][None]
+    pl.semaphore_wait(barrier, 20)
+
+    def send_info(step):
+        return pltpu.make_async_remote_copy(
+            src_ref=info.at[pts], dst_ref=info.at[pts], send_sem=info_send.at[step - 1], recv_sem=info_recv.at[step - 1],
+            device_id=(blk, mate(step)), device_id_type=pl.DeviceIdType.MESH,
+        )
+
+    for step in range(1, GROUP):
+        send_info(step).start()
+    load_win.wait()
+    load_feats.wait()
+    for rows in range(0, 1024, 256):
+        emb_ref[rows:rows + 256, :] = dot(feats[rows:rows + 256, :], win[...]).astype(jnp.bfloat16)
+    for step in range(1, GROUP):
+        send_info(step).wait()
+
+    lane = lax.broadcasted_iota(jnp.int32, (16, 128), 1)
+    for p in range(GROUP):
+        facts = info[p]
+        count = facts[:, 3:4]
+        listed = (lane >= 8) & (lane < 16) & ((lane - 8).astype(jnp.float32) < count)
+        times = []
+        for k in range(2):
+            hit = listed & (facts.astype(jnp.int32) == 2 * pts + k)
+            times.append(jnp.sum(jnp.where(hit, 1.0, 0.0), axis=1, keepdims=True) + jnp.zeros((16, 128), jnp.float32))
+        named = [send_ref[k:k + 1, p:p + 1] + jnp.zeros((16, 128), jnp.int32) for k in range(2)]
+        centre = [facts[:, n:n + 1] + jnp.zeros((16, 128), jnp.float32) for n in range(3)]
+        for t in range(8):
+            distance = 0.0
+            for n in range(3):
+                offset = pos_ref[n, t:t + 1, :].astype(jnp.float32) - centre[n]
+                distance = distance + offset * offset
+            often = jnp.where(named[0] == t, times[0], 0.0) + jnp.where(named[1] == t, times[1], 0.0)
+            pweights[16 * p:16 * p + 16, 128 * t:128 * t + 128] = (often / (1.0 + distance / 0.05)).astype(jnp.bfloat16)
+
+    outgoing[...] = dot(pweights[...], emb_ref[...]).astype(jnp.bfloat16).reshape(outgoing.shape)
+
+    def send_part(step):
+        return pltpu.make_async_remote_copy(
+            src_ref=outgoing.at[mate(step)], dst_ref=incoming.at[pts], send_sem=part_send.at[step - 1],
+            recv_sem=part_recv.at[step - 1], device_id=(blk, mate(step)), device_id_type=pl.DeviceIdType.MESH,
+        )
+
+    for step in range(1, GROUP):
+        send_part(step).start()
+    incoming[pl.ds(pts, 1)] = outgoing[pl.ds(pts, 1)]
+    for step in range(1, GROUP):
+        send_part(step).wait()
+    total = incoming[0].astype(jnp.float32)
+    for p in range(1, GROUP):
+        total = total + incoming[p].astype(jnp.float32)
+    pooled = total / turned[0:16, 3:4]
+    pooled_ref[...] = pooled
+    normed = rms(pooled).astype(jnp.bfloat16)
+    for part in range(3):
+        box_ref[part, x, y, z, core] = normed[:, 256 * part:256 * part + 256]
+
+    def box(part, spot, stage):
+        where = list(spot)
+        for earlier in range(stage):
+            where[(part + earlier) % 3] = slice(None)
+        return tuple(where)
+
+    def send_box(part, stage, step):
+        axis = (part + stage) % 3
+        view = box_ref.at[(part,) + box(part, place, stage) + (core,)]
+        return pltpu.make_async_remote_copy(
+            src_ref=view, dst_ref=view, send_sem=box_send.at[part, stage, step - 1], recv_sem=box_recv.at[part, stage, step - 1],
+            device_id=device(ring(axis, step), core), device_id_type=pl.DeviceIdType.MESH,
+        )
+
+    def send_twin(part, stage, step):
+        if stage == 0:
+            where, slot = box(part, place, 1), 0
+        else:
+            axis = (part + stage) % 3
+            where, slot = box(part, ring(axis, RING - step), stage), 3 * stage - 3 + step
+        view = box_ref.at[(part,) + where + (core,)]
+        return pltpu.make_async_remote_copy(
+            src_ref=view, dst_ref=view, send_sem=twin_send.at[part, slot], recv_sem=twin_recv.at[part, slot],
+            device_id=(blk, chip * 2 + 1 - core), device_id_type=pl.DeviceIdType.MESH,
+        )
+
+    order = (1, 3, 2)
+    for part in range(3):
+        for step in order:
+            send_box(part, 0, step).start()
+    for stage in range(1, 3):
+        for part in range(3):
+            for step in order:
+                send_box(part, stage - 1, step).wait_recv()
+            for step in order:
+                send_box(part, stage, step).start()
+            if stage == 1:
+                send_twin(part, 0, 0).start()
+            else:
+                for step in order:
+                    send_twin(part, 1, step).start()
+    for step in order:
+        for part in range(3):
+            send_box(part, 2, step).wait_recv()
+            send_twin(part, 2, step).start()
+    for part in range(3):
+        send_twin(part, 0, 0).wait()
+        for stage in range(3):
+            for step in order:
+                send_box(part, stage, step).wait_send()
+                if stage > 0:
+                    send_twin(part, stage, step).wait()
+
+
+def gather(feats, in_weight, point_pos, anchor_pos, send_tiles, nbr_slots, nbr_counts):
+    vmem = pl.BlockSpec(memory_space=pltpu.VMEM)
+    anywhere = pl.BlockSpec(memory_space=pl.ANY)
+    bf = jnp.bfloat16
+    dma = pltpu.SemaphoreType.DMA
+    return pl.pallas_call(
+        gather_kernel,
+        in_specs=[anywhere] * 2 + [vmem] * 5,
+        out_specs=[vmem] * 3,
+        out_shape=[
+            jax.ShapeDtypeStruct((1024, D), bf),
+            jax.ShapeDtypeStruct((16, D), jnp.float32),
+            jax.ShapeDtypeStruct((3, RING, RING, RING, CORES, 16, 256), bf),
+        ],
+        scratch_shapes=[
+            pltpu.VMEM((1024, D), bf), pltpu.VMEM((D, D), bf), pltpu.VMEM((128, 128), jnp.float32),
+            pltpu.VMEM((GROUP, 16, 128), jnp.float32), pltpu.VMEM((256, 1024), bf), pltpu.VMEM((GROUP, 16, D), bf),
+            pltpu.VMEM((GROUP, 16, D), bf), dma((2,)), dma((15,)), dma((15,)), dma((15,)), dma((15,)),
+            dma((3, 3, 3)), dma((3, 3, 3)), dma((3, 7)), dma((3, 7)),
+        ],
+        compiler_params=pltpu.CompilerParams(collective_id=0, has_side_effects=True, vmem_limit_bytes=40 * 2**20),
+    )(feats, in_weight, point_pos, anchor_pos, send_tiles, nbr_slots, nbr_counts)
+
+
 def body(point_feats, point_pos, anchor_pos, send_tiles, nbr_slots, nbr_counts, in_weight, q_weight, k_weight, v_weight,
          out_weight, up_weight, down_weight):
-    feats = point_feats.reshape(1024, D)
-    me = lax.axis_index("pts")
-    counts = nbr_counts.astype(jnp.float32)
-    info = jnp.concatenate([anchor_pos.T, counts[:, None], nbr_slots.astype(jnp.float32)], axis=1)
-    info = lax.all_gather(info, "pts", axis=0, tiled=True)
-    emb = dot(feats, in_weight).astype(jnp.bfloat16)
-    slots = info[:, 4:12]
-    live = jnp.arange(8, dtype=jnp.float32)[None, :] < info[:, 3:4]
-    base = (2 * me).astype(jnp.float32)
-    sent = jnp.repeat(send_tiles[0], 16, axis=0)
-    tiles = jnp.arange(8, dtype=jnp.int32)[None, :]
-    counted = 0.0
-    for k in range(2):
-        times = jnp.sum(((slots == base + k) & live).astype(jnp.float32), axis=1, keepdims=True)
-        counted = counted + jnp.where(sent[:, k:k + 1] == tiles, times, 0.0)
-    places = point_pos.astype(jnp.float32)
-    offsets = places[None] - info[:, None, 0:3, None]
-    distance = jnp.sum(offsets * offsets, axis=2)
-    weights = (counted[:, :, None] / (1.0 + distance / 0.05)).reshape(256, 1024).astype(jnp.bfloat16)
-    partial = dot(weights, emb).astype(jnp.bfloat16)
-    arrived = lax.all_to_all(partial.reshape(16, 16, D), "pts", split_axis=0, concat_axis=0, tiled=True)
-    pooled = jnp.sum(arrived.astype(jnp.float32), axis=0) / counts[:, None]
-    normed = rms(pooled).astype(jnp.bfloat16)
-    gathered = lax.all_gather(normed, ("blk", "pts"), axis=0, tiled=True)
-    anchors, points = compute(emb, pooled, gathered, q_weight, k_weight, v_weight, out_weight, up_weight, down_weight)
+    emb, pooled, boxes = gather(
+        point_feats.reshape(1024, D), in_weight, jnp.transpose(point_pos, (1, 0, 2)), anchor_pos, send_tiles[0].T, nbr_slots.T,
+        nbr_counts[None],
+    )
+    anchors, points = compute(
+        emb, pooled, boxes.reshape(3, A, 256), q_weight, k_weight, v_weight, out_weight, up_weight, down_weight
+    )
     return anchors, points.reshape(8, 128, D)
 
 

time: 183 us -> 112 us (0.61)
  waiting for transfers between devices: 65.9 us -> 0 us
  Pallas kernels: 60.7 us -> 101 us
  blocking collectives: 33.7 us -> 0 us
  between operations: 14.2 us -> 0.83 us
  local copies, waits for them, and re-layouts: 1.27 us -> 9.45 us
  other arithmetic: 5.41 us -> 0 us
  matrix products: 1.98 us -> 0 us
    all_gather x1 -> x0, waiting for transfers between devices: 65.9 us -> none  [body(): gathered = lax.all_gather(normed, ('blk', 'pts'), axis=0, tiled=True)]
    pallas_call x0 -> x1, Pallas kernels: none -> 40.3 us  [gather(): pl.pallas_call(gather_kernel, in_specs=[anywhere] * 2 + [vmem] * 5, out_s...]
    all_gather x1 -> x0, blocking collectives: 22.6 us -> none  [body(): info = lax.all_gather(info, 'pts', axis=0, tiled=True)]
    all_to_all x1 -> x0, blocking collectives: 11.1 us -> none  [body(): lax.all_to_all(partial.reshape(16, 16, D), 'pts', split_axis=0, concat_ax...]
    unnamed x9 -> x20, local copies, waits for them, and re-layouts: 0.08 us -> 9.45 us
    convert_element_type x5 -> x0, other arithmetic: 3.17 us -> none  [the longest x1 0.77 us: body(): counts = nbr_counts.astype(jnp.float32)]
    dot_general x2 -> x0, matrix products: 1.98 us -> none  [dot(): return jnp.dot(a, b, preferred_element_type=jnp.float32)]
  transfers between devices with their start and end apart: 1 -> 0, of which waited for: 1 -> 0; matrix products, arithmetic and copies ran while one was open for 0% -> 0% of each run, Pallas kernels for 0% -> 0%
where the time goes in v2:
time: 112 us; the launch traced here: 111 us
  Pallas kernels  101 us (90%)
  local copies, waits for them, and re-layouts  9.45 us (8%)
    pallas_call x1, Pallas kernels, compute(): pl.pallas_call(kern, grid=(n,), in_specs=[full, full, full] + [anys] * 6,...  60.7 us
    pallas_call x1, Pallas kernels, gather(): pl.pallas_call(gather_kernel, in_specs=[anywhere] * 2 + [vmem] * 5, out_s...  40.3 us
    unnamed x20, local copies, waits for them, and re-layouts  9.45 us

profile of v2, /device:TPU:1, one launch (start us, length us, event | category | flops | bytes accessed | tf_op | source)
XLA Modules:
  0.0 111.3 jit_solution(16856840438651773192)
XLA Ops:
  0.6 0.0 copy-start.1
  0.6 1.4 %copy-done.1 = bf16[8,128,768]{2,1,0:T(8,128)(2,1)S(1)} copy-done((bf16[8,128,768]{2,1,0:T(8,128)(2,1)S(1)}, bf16[8,128,768]{2,1,0:T(8,128)(2,1)}, u32[]{:S(2)}) %copy-start.1) | copy-done | bytes 1572888
  2.0 0.0 copy-start.3
  2.0 1.3 %copy-done.3 = bf16[768,768]{1,0:T(8,128)(2,1)S(1)} copy-done((bf16[768,768]{1,0:T(8,128)(2,1)S(1)}, bf16[768,768]{1,0:T(8,128)(2,1)}, u32[]{:S(2)}) %copy-start.3) | copy-done | bytes 1179672
  3.3 0.0 copy-start.5
  3.3 0.7 copy-done.5
  4.0 0.0 copy-start.6
  4.0 0.7 copy-done.6
  4.7 0.0 copy-start.7
  4.7 0.7 copy-done.7
  5.4 0.0 copy-start.8
  5.4 0.7 copy-done.8
  6.1 0.0 copy-start.9
  6.1 0.7 copy-done.9
  6.7 40.3 %shard_map.140 = (bf16[1024,768]{1,0:T(8,128)(2,1)S(1)}, f32[16,768]{1,0:T(8,128)S(1)}, bf16[3,4,4,4,2,16,256]{6,5,4,3,2,1,0:T(8,128)(2,1)S(1)}) custom-call(bf16[1024,768]{1,0:T(8,128)(2,1)S(1)} %bitcast.10, bf16[768,768]{1,0:T(8,128)(2,1)S(1)} %copy-done.3, bf16[3,8,128]{2,1,0:T(8,128)(2,1)S(1)} %bitcast.11, f32[3,16]{1,0:T(4,128)S(1)} %copy-done.7, ...), custom_call_target="tpu_custom_call" | custom-call | tf_op jit(solution)/shard_map/pallas_call | solution.py:292
  47.0 0.0 copy-start
  47.0 1.6 %copy-done = bf16[3,4,4,4,2,16,256]{6,5,4,3,2,1,0:T(8,128)(2,1)} copy-done((bf16[3,4,4,4,2,16,256]{6,5,4,3,2,1,0:T(8,128)(2,1)}, bf16[3,4,4,4,2,16,256]{6,5,4,3,2,1,0:T(8,128)(2,1)S(1)}, u32[]{:S(2)}) %copy-start) | copy-done | bytes 3145752
  48.6 0.0 copy-start.2
  48.6 1.1 %copy-done.2 = bf16[1024,768]{1,0:T(8,128)(2,1)} copy-done((bf16[1024,768]{1,0:T(8,128)(2,1)}, bf16[1024,768]{1,0:T(8,128)(2,1)S(1)}, u32[]{:S(2)}) %copy-start.2) | copy-done | bytes 1572888
  49.8 0.0 copy-start.4
  49.8 0.6 copy-done.4
  50.4 60.7 %shard_map.141 = (f32[16,768]{1,0:T(8,128)}, f32[1024,768]{1,0:T(8,128)}) custom-call(bf16[1024,768]{1,0:T(8,128)(2,1)} %copy-done.2, f32[16,768]{1,0:T(8,128)} %copy-done.4, bf16[3,2048,256]{2,1,0:T(8,128)(2,1)} %bitcast.9, bf16[768,768]{1,0:T(8,128)(2,1)} %wq_h.1, bf16[768,768]{1,0:T(8,128)(2,1)} %wk_h.1, bf16[768,768]{1,0:T(8,128)(2,1)} %wv_h.1, ...), custom_call_target="tpu_custom_call" | custom-call | tf_op jit(solution)/shard_map/pallas_call | solution.py:110
Async XLA Ops:
  0.6 1.4 %copy-start.1 = (bf16[8,128,768]{2,1,0:T(8,128)(2,1)S(1)}, bf16[8,128,768]{2,1,0:T(8,128)(2,1)}, u32[]{:S(2)}) copy-start(bf16[8,128,768]{2,1,0:T(8,128)(2,1)} %param.13) | copy-start | bytes 4718596
  2.0 1.3 %copy-start.3 = (bf16[768,768]{1,0:T(8,128)(2,1)S(1)}, bf16[768,768]{1,0:T(8,128)(2,1)}, u32[]{:S(2)}) copy-start(bf16[768,768]{1,0:T(8,128)(2,1)} %win_hbm.1) | copy-start | bytes 3538948
  3.3 0.7 copy-start.5
  4.0 0.7 copy-start.6
  4.7 0.7 copy-start.7
  5.4 0.7 copy-start.8
  6.1 0.7 copy-start.9
  47.0 1.6 %copy-start = (bf16[3,4,4,4,2,16,256]{6,5,4,3,2,1,0:T(8,128)(2,1)}, bf16[3,4,4,4,2,16,256]{6,5,4,3,2,1,0:T(8,128)(2,1)S(1)}, u32[]{:S(2)}) copy-start(bf16[3,4,4,4,2,16,256]{6,5,4,3,2,1,0:T(8,128)(2,1)S(1)} %get-tuple-element.9) | copy-start | bytes 9437188
  48.6 1.1 %copy-start.2 = (bf16[1024,768]{1,0:T(8,128)(2,1)}, bf16[1024,768]{1,0:T(8,128)(2,1)S(1)}, u32[]{:S(2)}) copy-start(bf16[1024,768]{1,0:T(8,128)(2,1)S(1)} %get-tuple-element.7.emb) | copy-start | bytes 4718596
  49.8 0.6 copy-start.4

commit v3 on v1

v3 whole, which is shorter than its diff:
```python
import jax
import jax.numpy as jnp
from jax import lax
from jax.experimental import pallas as pl
from jax.experimental.pallas import tpu as pltpu
from jax.sharding import PartitionSpec as P

HEADS = 12
HD = 64
D = 768
FFH = 3072
A = 2048
POINTS = 1024
ROWS = 208
EPS = 1e-6
LOG2E = 1.4426950408889634
CORES = 2
RING = 4
GROUP = 16
MESH = pl.DeviceIdType.MESH
BF = jnp.bfloat16
F32 = jnp.float32
MATES = [(1, 2, 0), (1, 2, 1), (1, 1, 0), (1, 3, 0), (1, 1, 1), (1, 3, 1), (0, 2, 0), (0, 2, 1),
         (1, 0, 0), (1, 0, 1), (0, 1, 0), (0, 3, 0), (0, 1, 1), (0, 3, 1), (0, 0, 1)]


def rms(rows):
    return rows * lax.rsqrt(jnp.mean(rows * rows, axis=-1, keepdims=True) + EPS)


def dot(left, right):
    return jnp.dot(left, right, preferred_element_type=F32)


def queries_of(rows, weight):
    return (dot(rms(rows).astype(BF), weight) * (LOG2E / 8.0)).astype(BF)


def gather_kernel(
    feats_hbm, win_hbm, wq_hbm, wk_hbm, wv_hbm, pos_hbm, apos_hbm, send_hbm, slots_hbm, counts_hbm,
    emb_ref, pooled_ref, q_ref, kt_ref, v_ref,
    feats, win, wq, wk, wv, pos_ref, apos_ref, send_ref, slots_ref, counts_ref,
    turn, info, pweights, outgoing, incoming, box_ref,
    local_sem, info_send, info_recv, part_send, part_recv,
    line_send, line_recv, plane_send, plane_recv, cube_send, cube_recv, twin_send, twin_recv,
):
    blk = lax.axis_index("blk")
    pts = lax.axis_index("pts")
    x, y_hi = blk // 2, lax.rem(blk, 2)
    core = lax.rem(pts, 2)
    chip = pts // 2
    z, y_lo = lax.rem(chip, 4), chip // 4
    y = y_hi * 2 + y_lo
    place = (x, y, z)

    def device(spot):
        return (spot[0] * 2 + spot[1] // 2, (lax.rem(spot[1], 2) * 4 + spot[2]) * 2 + core)

    def ring(axis, step):
        spot = list(place)
        spot[axis] = lax.rem(place[axis] + step, RING)
        return tuple(spot)

    def mate(n):
        dy, dz, dc = MATES[n]
        return (lax.rem(y_lo + dy, 2) * 4 + lax.rem(z + dz, RING)) * 2 + lax.rem(core + dc, 2)

    loads = [
        pltpu.make_async_copy(source, target, local_sem.at[n])
        for n, (source, target) in enumerate((
            (feats_hbm, feats), (win_hbm, win), (apos_hbm, apos_ref), (slots_hbm, slots_ref), (counts_hbm, counts_ref),
            (wq_hbm, wq), (send_hbm, send_ref), (pos_hbm, pos_ref), (wk_hbm, wk), (wv_hbm, wv)))
    ]
    for load in loads:
        load.start()

    barrier = pltpu.get_barrier_semaphore()

    def greet(device_id):
        pl.semaphore_signal(barrier, inc=1, device_id=device_id, device_id_type=MESH)

    for n in range(GROUP - 1):
        greet((blk, mate(n)))
    for step in range(1, RING):
        greet(device(ring(0, step)))
    across = lax.rem(y_hi + 1, 2)
    for low in range(2):
        greet((x * 2 + across, (low * 4 + z) * 2 + core))

    for n in range(2, 5):
        loads[n].wait()
    turn[...] = jnp.zeros_like(turn)
    turn[0:3, 0:16] = apos_ref[...]
    turn[3:4, 0:16] = counts_ref[...].astype(F32)
    turn[8:16, 0:16] = slots_ref[...].astype(F32)
    turned = turn[...].T[0:16, :]
    info[pl.ds(pts, 1)] = turned[None]
    loads[0].wait()
    loads[1].wait()
    for rows in range(0, POINTS, 256):
        emb_ref[rows:rows + 256, :] = dot(feats[rows:rows + 256, :], win[...]).astype(BF)

    pl.semaphore_wait(barrier, 20)

    def send_info(n):
        return pltpu.make_async_remote_copy(
            src_ref=info.at[pts], dst_ref=info.at[pts], send_sem=info_send.at[n], recv_sem=info_recv.at[n],
            device_id=(blk, mate(n)), device_id_type=MESH,
        )

    for n in range(GROUP - 1):
        send_info(n).start()
    for n in range(5, 8):
        loads[n].wait()
    for rows in range(0, POINTS, 256):
        q_ref[rows:rows + 256, :] = queries_of(emb_ref[rows:rows + 256, :].astype(F32), wq[...])
    for n in range(GROUP - 1):
        send_info(n).wait()

    lane = lax.broadcasted_iota(jnp.int32, (16, 128), 1)
    for p in range(GROUP):
        facts = info[p]
        count = facts[:, 3:4]
        listed = (lane >= 8) & (lane < 16) & ((lane - 8).astype(F32) < count)
        times = []
        for k in range(2):
            hit = listed & (facts.astype(jnp.int32) == 2 * pts + k)
            times.append(jnp.sum(jnp.where(hit, 1.0, 0.0), axis=1, keepdims=True) + jnp.zeros((16, 128), F32))
        named = [send_ref[k:k + 1, p:p + 1] + jnp.zeros((16, 128), jnp.int32) for k in range(2)]
        centre = [facts[:, n:n + 1] + jnp.zeros((16, 128), F32) for n in range(3)]
        for t in range(8):
            distance = 0.0
            for n in range(3):
                offset = pos_ref[n, t:t + 1, :].astype(F32) - centre[n]
                distance = distance + offset * offset
            often = jnp.where(named[0] == t, times[0], 0.0) + jnp.where(named[1] == t, times[1], 0.0)
            pweights[16 * p:16 * p + 16, 128 * t:128 * t + 128] = (often / (1.0 + distance / 0.05)).astype(BF)

    outgoing[...] = dot(pweights[...], emb_ref[...]).astype(BF).reshape(outgoing.shape)

    def send_part(n):
        return pltpu.make_async_remote_copy(
            src_ref=outgoing.at[mate(n)], dst_ref=incoming.at[pts], send_sem=part_send.at[n], recv_sem=part_recv.at[n],
            device_id=(blk, mate(n)), device_id_type=MESH,
        )

    for n in range(GROUP - 1):
        send_part(n).start()
    incoming[pl.ds(pts, 1)] = outgoing[pl.ds(pts, 1)]
    loads[8].wait()
    loads[9].wait()
    wk[...] = wk[...].T
    for n in range(GROUP - 1):
        send_part(n).wait()
    total = incoming[0].astype(F32)
    for p in range(1, GROUP):
        total = total + incoming[p].astype(F32)
    pooled = total / turned[:, 3:4]
    normed = rms(pooled).astype(BF)
    for part in range(3):
        box_ref[part, core, x, y, z] = normed[:, 256 * part:256 * part + 256]

    def axis_of(part, stage):
        return (part + stage) % 3

    def view(part, spot, free):
        where = list(spot)
        for stage in range(free):
            where[axis_of(part, stage)] = slice(None)
        return box_ref.at[(part, core) + tuple(where)]

    def send_line(part, step):
        block = view(part, place, 0)
        return pltpu.make_async_remote_copy(
            src_ref=block, dst_ref=block, send_sem=line_send.at[part, step], recv_sem=line_recv.at[part, step],
            device_id=device(ring(axis_of(part, 0), step)), device_id_type=MESH,
        )

    def send_plane(part, step):
        line = view(part, place, 1)
        return pltpu.make_async_remote_copy(
            src_ref=line, dst_ref=line, send_sem=plane_send.at[part, step], recv_sem=plane_recv.at[part, step],
            device_id=device(ring(axis_of(part, 1), step)), device_id_type=MESH,
        )

    def send_cube(part, piece, step):
        line = view(part, ring(axis_of(part, 1), (RING - piece) % RING), 1)
        return pltpu.make_async_remote_copy(
            src_ref=line, dst_ref=line, send_sem=cube_send.at[part, piece, step], recv_sem=cube_recv.at[part, piece, step],
            device_id=device(ring(axis_of(part, 2), step)), device_id_type=MESH,
        )

    def send_twin(part, slot):
        if slot < 4:
            block = view(part, ring(axis_of(part, 1), (RING - slot) % RING), 1)
        else:
            block = view(part, ring(axis_of(part, 2), RING + 3 - slot), 2)
        return pltpu.make_async_remote_copy(
            src_ref=block, dst_ref=block, send_sem=twin_send.at[part, slot], recv_sem=twin_recv.at[part, slot],
            device_id=(blk, chip * 2 + 1 - core), device_id_type=MESH,
        )

    steps = (2, 1, 3)
    for part in range(3):
        for step in steps:
            send_line(part, step).start()
    pooled_ref[...] = pooled
    q_ref[POINTS:POINTS + 16, :] = queries_of(pooled, wq[...])
    for part in range(3):
        for step in (1, 3, 2):
            send_line(part, step).wait_recv()
        for step in steps:
            send_plane(part, step).start()
        for step in steps:
            send_cube(part, 0, step).start()
        send_twin(part, 0).start()
    for piece in (1, 3, 2):
        for part in range(3):
            send_plane(part, piece).wait_recv()
            for step in steps:
                send_cube(part, piece, step).start()
            send_twin(part, piece).start()
    for step in (1, 3, 2):
        for part in range(3):
            for piece in (0, 1, 3, 2):
                send_cube(part, piece, step).wait_recv()
            send_twin(part, 3 + step).start()

    def project(half, first):
        blocks = [box_ref[part, half].reshape(A // 2, 256) for part in range(3)]
        for c in range(0, A // 2, 256):
            keys = None
            values = None
            for part in range(3):
                block = blocks[part][c:c + 256]
                columns = slice(256 * part, 256 * part + 256)
                key = lax.dot_general(wk[:, columns], block, (((1,), (1,)), ((), ())), preferred_element_type=F32)
                value = dot(block, wv[columns, :])
                keys = key if keys is None else keys + key
                values = value if values is None else values + value
            kt_ref[:, first + c:first + c + 256] = keys.astype(BF)
            v_ref[first + c:first + c + 256, :] = values.astype(BF)

    project(core, 0)
    for part in range(3):
        for slot in range(7):
            send_twin(part, slot).wait()
    project(1 - core, A // 2)
    for part in range(3):
        for step in steps:
            send_line(part, step).wait_send()
            send_plane(part, step).wait_send()
            for piece in range(RING):
                send_cube(part, piece, step).wait_send()


def gather(feats, in_weight, q_weight, k_weight, v_weight, point_pos, anchor_pos, send_tiles, nbr_slots, nbr_counts):
    vmem = pl.BlockSpec(memory_space=pltpu.VMEM)
    hbm = pl.BlockSpec(memory_space=pltpu.HBM)
    dma = pltpu.SemaphoreType.DMA
    square = pltpu.VMEM((D, D), BF)
    return pl.pallas_call(
        gather_kernel,
        in_specs=[hbm] * 10,
        out_specs=[vmem] * 5,
        out_shape=[
            jax.ShapeDtypeStruct((POINTS, D), BF), jax.ShapeDtypeStruct((16, D), F32), jax.ShapeDtypeStruct((POINTS + 16, D), BF),
            jax.ShapeDtypeStruct((D, A), BF), jax.ShapeDtypeStruct((A, D), BF),
        ],
        scratch_shapes=[
            pltpu.VMEM((POINTS, D), BF), square, square, square, square,
            pltpu.VMEM(point_pos.shape, BF), pltpu.VMEM(anchor_pos.shape, F32), pltpu.VMEM(send_tiles.shape, jnp.int32),
            pltpu.VMEM(nbr_slots.shape, jnp.int32), pltpu.VMEM(nbr_counts.shape, jnp.int32),
            pltpu.VMEM((128, 128), F32), pltpu.VMEM((GROUP, 16, 128), F32), pltpu.VMEM((256, POINTS), BF),
            pltpu.VMEM((GROUP, 16, D), BF), pltpu.VMEM((GROUP, 16, D), BF),
            pltpu.VMEM((3, CORES, RING, RING, RING, 16, 256), BF),
            dma((10,)), dma((15,)), dma((15,)), dma((15,)), dma((15,)),
            dma((3, 4)), dma((3, 4)), dma((3, 4)), dma((3, 4)), dma((3, 4, 4)), dma((3, 4, 4)), dma((3, 7)), dma((3, 7)),
        ],
        compiler_params=pltpu.CompilerParams(collective_id=0, has_side_effects=True, vmem_limit_bytes=28 * 2**20),
    )(*[
        pltpu.with_memory_space_constraint(operand, pltpu.HBM)
        for operand in (feats, in_weight, q_weight, k_weight, v_weight, point_pos, anchor_pos, send_tiles, nbr_slots, nbr_counts)
    ])


def block_kernel(
    emb, pooled, queries, kt, values, wo_hbm, wu_hbm, wd_hbm, anchors_hbm, points_hbm,
    wo, wu, wd, augmented, stream, finished, attended, sems, out_sems,
):
    i = pl.program_id(0)
    n = pl.num_programs(0)
    loads = [
        pltpu.make_async_copy(source, target, sems.at[k])
        for k, (source, target) in enumerate(((wo_hbm, wo), (wu_hbm, wu), (wd_hbm, wd)))
    ]

    def store(step, slot):
        return pltpu.make_async_copy(finished.at[slot], points_hbm.at[pl.ds(step * ROWS, ROWS)], out_sems.at[slot])

    @pl.when(i == 0)
    def _():
        for load in loads:
            load.start()
        low = lax.broadcasted_iota(jnp.int32, (256, 128), 1) < HD
        one = jnp.ones((256, 128), BF)
        zero = jnp.zeros((256, 128), BF)
        for c in range(0, A, 256):
            rows = slice(c, c + 256)
            for p in range(HEADS // 2):
                pair = values[rows, 128 * p:128 * p + 128]
                augmented[2 * p, rows, 0:128] = jnp.where(low, pair, zero)
                augmented[2 * p, rows, 128:256] = jnp.where(low, one, zero)
                augmented[2 * p + 1, rows, 0:128] = jnp.where(low, zero, pair)
                augmented[2 * p + 1, rows, 128:256] = jnp.where(low, zero, one)

    @pl.when(i < n - 1)
    def _():
        stream[...] = emb[pl.ds(pl.multiple_of(i * ROWS, 16), ROWS), :].astype(F32)

    @pl.when(i == n - 1)
    def _():
        stream[0:ROWS - 16, :] = emb[POINTS - (ROWS - 16):POINTS, :].astype(F32)
        stream[ROWS - 16:ROWS, :] = pooled[...]

    here = pl.ds(pl.multiple_of(i * ROWS, 16), ROWS)
    low = lax.broadcasted_iota(jnp.int32, (ROWS, 128), 1) < HD
    for p in range(HEADS // 2):
        pair = queries[here, 128 * p:128 * p + 128]
        zero = jnp.zeros_like(pair)
        out = jnp.zeros((ROWS, 256), F32)
        for a in range(2):
            query = jnp.where(low, pair, zero) if a == 0 else jnp.where(low, zero, pair)
            scores = dot(query, kt[128 * p:128 * p + 128, :])
            largest = jnp.max(scores, axis=1, keepdims=True)
            weights = jnp.exp2(scores - largest).astype(BF)
            out = out + dot(weights, augmented[2 * p + a, :, :])
        attended[:, 128 * p:128 * p + 128] = (out[:, 0:128] / out[:, 128:256]).astype(BF)

    @pl.when(i == 0)
    def _():
        for load in loads:
            load.wait()

    residual = stream[...] + dot(attended[...], wo[...])
    normed = rms(residual).astype(BF)
    result = residual
    for c in range(0, FFH, 768):
        hidden = jax.nn.gelu(dot(normed, wu[:, c:c + 768])).astype(BF)
        result = result + dot(hidden, wd[c:c + 768, :])
    slot = lax.rem(i, 2)

    @pl.when(i >= 2)
    def _():
        store(i - 2, slot).wait()

    finished[slot] = result

    @pl.when(i < n - 1)
    def _():
        store(i, slot).start()

    @pl.when(i == n - 1)
    def _():
        last = ROWS - 16
        tail = pltpu.make_async_copy(
            finished.at[slot, pl.ds(0, last)], points_hbm.at[pl.ds(POINTS - last, last)], out_sems.at[2])
        anchors = pltpu.make_async_copy(finished.at[slot, pl.ds(last, 16)], anchors_hbm, out_sems.at[3])
        tail.start()
        anchors.start()
        store(i - 1, 1 - slot).wait()
        tail.wait()
        anchors.wait()


def block(emb, pooled, queries, kt, values, out_weight, up_weight, down_weight):
    vmem = pl.BlockSpec(memory_space=pltpu.VMEM)
    hbm = pl.BlockSpec(memory_space=pltpu.HBM)
    return pl.pallas_call(
        block_kernel,
        grid=((POINTS + 16) // ROWS,),
        in_specs=[vmem] * 5 + [hbm] * 3,
        out_specs=[hbm, hbm],
        out_shape=[jax.ShapeDtypeStruct((16, D), F32), jax.ShapeDtypeStruct((POINTS, D), F32)],
        scratch_shapes=[
            pltpu.VMEM((D, D), BF), pltpu.VMEM((D, FFH), BF), pltpu.VMEM((FFH, D), BF), pltpu.VMEM((HEADS, A, 256), BF),
            pltpu.VMEM((ROWS, D), F32), pltpu.VMEM((2, ROWS, D), F32), pltpu.VMEM((ROWS, D), BF),
            pltpu.SemaphoreType.DMA((3,)), pltpu.SemaphoreType.DMA((4,)),
        ],
        compiler_params=pltpu.CompilerParams(vmem_limit_bytes=38 * 2**20, dimension_semantics=("arbitrary",)),
    )(emb, pooled, queries, kt, values, out_weight, up_weight, down_weight)


def body(point_feats, point_pos, anchor_pos, send_tiles, nbr_slots, nbr_counts, in_weight, q_weight, k_weight, v_weight,
         out_weight, up_weight, down_weight):
    emb, pooled, queries, kt, values = gather(
        point_feats.reshape(POINTS, D), in_weight, q_weight, k_weight, v_weight, jnp.transpose(point_pos, (1, 0, 2)),
        anchor_pos, send_tiles[0].T, nbr_slots.T, nbr_counts[None],
    )
    anchors, points = block(emb, pooled, queries, kt, values, out_weight, up_weight, down_weight)
    return anchors, points.reshape(POINTS // 128, 128, D)


def solution(mesh):
    both = ("blk", "pts")
    return jax.shard_map(
        body,
        mesh=mesh,
        in_specs=(P(both, None, None), P(both, None, None), P(None, both), P(both, None, None), P(both, None), P(both))
        + (P(),) * 7,
        out_specs=(P(both, None), P(both, None, None)),
        check_vma=False,
    )
```

time: 183 us -> 97.3 us (0.53)
  waiting for transfers between devices: 65.9 us -> 0 us
  Pallas kernels: 60.7 us -> 95.9 us
  blocking collectives: 33.7 us -> 0 us
  between operations: 14.2 us -> 0.83 us
  other arithmetic: 5.41 us -> 0 us
  matrix products: 1.98 us -> 0 us
    all_gather x1 -> x0, waiting for transfers between devices: 65.9 us -> none  [body(): gathered = lax.all_gather(normed, ('blk', 'pts'), axis=0, tiled=True)]
    pallas_call x1 -> x2, Pallas kernels: 60.7 us -> 95.9 us  [the longest x1 52.9 us: block(): pl.pallas_call(block_kernel, grid=((POINTS + 16) // ROWS,), in_specs=[vme...]
    all_gather x1 -> x0, blocking collectives: 22.6 us -> none  [body(): info = lax.all_gather(info, 'pts', axis=0, tiled=True)]
    all_to_all x1 -> x0, blocking collectives: 11.1 us -> none  [body(): lax.all_to_all(partial.reshape(16, 16, D), 'pts', split_axis=0, concat_ax...]
    convert_element_type x5 -> x0, other arithmetic: 3.17 us -> none  [the longest x1 0.77 us: body(): counts = nbr_counts.astype(jnp.float32)]
    dot_general x2 -> x0, matrix products: 1.98 us -> none  [dot(): return jnp.dot(a, b, preferred_element_type=jnp.float32)]
  transfers between devices with their start and end apart: 1 -> 0, of which waited for: 1 -> 0; matrix products, arithmetic and copies ran while one was open for 0% -> 0% of each run, Pallas kernels for 0% -> 0%
where the time goes in v3:
time: 97.3 us; the launch traced here: 96.7 us
  Pallas kernels  95.9 us (99%)
    pallas_call x1, Pallas kernels, block(): pl.pallas_call(block_kernel, grid=((POINTS + 16) // ROWS,), in_specs=[vme...  52.9 us
    pallas_call x1, Pallas kernels, gather(): pl.pallas_call(gather_kernel, in_specs=[hbm] * 10, out_specs=[vmem] * 5,...  42.9 us

profile of v3, /device:TPU:1, one launch (start us, length us, event | category | flops | bytes accessed | tf_op | source)
XLA Modules:
  0.0 96.7 jit_solution(1067180991619256106)
XLA Ops:
  0.6 0.0 copy-start
  0.6 0.0 copy-start.1
  0.7 42.9 %shard_map.140 = (bf16[1024,768]{1,0:T(8,128)(2,1)S(1)}, f32[16,768]{1,0:T(8,128)S(1)}, bf16[1040,768]{1,0:T(8,128)(2,1)S(1)}, bf16[768,2048]{1,0:T(8,128)(2,1)S(1)}, bf16[2048,768]{1,0:T(8,128)(2,1)S(1)}) custom-call(bf16[1024,768]{1,0:T(8,128)(2,1)} %bitcast.8, bf16[768,768]{1,0:T(8,128)(2,1)} %win_hbm.1, bf16[768,768]{1,0:T(8,128)(2,1)} %wq_hbm.1, ...), custom_call_target="tpu_custom_call" | custom-call | tf_op jit(solution)/shard_map/pallas_call | solution.py:262
  43.6 0.0 copy-done
  43.6 0.0 copy-done.1
  43.6 52.9 %shard_map.141 = (f32[16,768]{1,0:T(8,128)}, f32[1024,768]{1,0:T(8,128)}) custom-call(bf16[1024,768]{1,0:T(8,128)(2,1)S(1)} %get-tuple-element.9.emb, f32[16,768]{1,0:T(8,128)S(1)} %get-tuple-element.10.pooled, bf16[1040,768]{1,0:T(8,128)(2,1)S(1)} %get-tuple-element.11.queries, bf16[768,2048]{1,0:T(8,128)(2,1)S(1)} %get-tuple-element.12.kt, ...), custom_call_target="tpu_custom_call" | custom-call | tf_op jit(solution)/shard_map/pallas_call | solution.py:379
Async XLA Ops:
  0.6 43.0 %copy-start = (bf16[768,3072]{1,0:T(8,128)(2,1)S(1)}, bf16[768,3072]{1,0:T(8,128)(2,1)}, u32[]{:S(2)}) copy-start(bf16[768,3072]{1,0:T(8,128)(2,1)} %wu_hbm.1) | copy-start | bytes 14155780
  0.6 43.0 %copy-start.1 = (bf16[768,768]{1,0:T(8,128)(2,1)S(1)}, bf16[768,768]{1,0:T(8,128)(2,1)}, u32[]{:S(2)}) copy-start(bf16[768,768]{1,0:T(8,128)(2,1)} %wo_hbm.1) | copy-start | bytes 3538948
